TPU v7x, 128 devices: a whole 4x4x4 slice. The times are simulated.
128 devices in a mesh: grp: 8 (over x, y_hi), dev: 16 (over y_lo, z, core).
Axes of the slice: x: 4, y: 4 (y_hi: 2, y_lo: 2; y = y_hi * 2 + y_lo), z: 4, core: 2. Of those that a mesh axis runs over, the one named last changes fastest.
Arguments:
- batch_rows: bfloat16 [4096, 512], P(('grp', 'dev')), may hold values from -30 to 30
- batch_labels: int32 [4096], P(('grp', 'dev')), may hold values from 0 to 1023, as said below
- memory: bfloat16 [262144, 512], P(('grp', 'dev')), may hold values from -30 to 30
- memory_labels: int32 [262144], P(('grp', 'dev')), may hold values from 0 to 1023
- keep_bits: int32 [262144], P(('grp', 'dev')), may hold values from 0 to 1
- step_index: int32 [1], replicated, may hold values from 0 to 999999
Outputs:
- grad_batch: float32 [4096, 512], P(('grp', 'dev'))
- anchor_loss: float32 [4096], P(('grp', 'dev'))
- new_memory: bfloat16 [262144, 512], P(('grp', 'dev'))
- new_labels: int32 [262144], P(('grp', 'dev'))
Inputs may be any that keep to these rules, and one draw needn't show every extreme that they name: `batch_labels`: labels of batch and memory rows are class numbers below 1024.
All inputs are finite; a program needn't handle non-finite values.
Results may differ from a plain program's by a relative error of at most 0.0034.
Values may be sent and summed in bfloat16 or wider, within the bound.
A program may use at most 128 MiB of HBM per device.

v0:
```python
import jax
import jax.numpy as jnp
from jax import lax
from jax.sharding import PartitionSpec as P

pos_scale = 2.0
neg_scale = 50.0
margin = 0.5


def normalize(values):
    floats = values.astype(jnp.float32)
    radius = jnp.sqrt(jnp.sum(floats * floats, axis=1, keepdims=True) + 1e-06)
    return (floats / radius, radius)


def per_device(batch_rows, batch_labels, memory, memory_labels, keep_bits, step_index):
    group_size = lax.axis_size("dev")
    devices_all = lax.axis_size("grp") * group_size
    my_index = lax.axis_index("grp") * group_size + lax.axis_index("dev")
    local_rows = batch_rows.shape[0]
    width = batch_rows.shape[1]
    unit_rows, radius = normalize(batch_rows)
    local_anchors = unit_rows.astype(jnp.bfloat16)
    anchors, labels_all = (
        lax.all_gather(local_anchors, ("grp", "dev"), axis=0, tiled=True),
        lax.all_gather(batch_labels, ("grp", "dev"), axis=0, tiled=True),
    )
    memory_keys = normalize(memory)[0].astype(jnp.bfloat16)
    kept_rows = (keep_bits > 0)[None, :]
    row_count = anchors.shape[0]
    block_rows = min(512, row_count)
    blocks = row_count // block_rows

    def score_block(inputs):
        block_anchors, block_labels = inputs
        scores = lax.dot_general(
            block_anchors, memory_keys, (((1,), (1,)), ((), ())), preferred_element_type=jnp.float32
        )
        same_class = block_labels[:, None] == memory_labels[None, :]
        positive = jnp.logical_and(same_class, kept_rows)
        negative = jnp.logical_and(jnp.logical_not(same_class), kept_rows)
        pos_term = jnp.where(positive, jnp.exp(-pos_scale * (scores - margin)), 0.0)
        neg_term = jnp.where(negative, jnp.exp(neg_scale * (scores - margin)), 0.0)
        pull = jnp.dot(
            pos_term.astype(jnp.bfloat16), memory_keys, preferred_element_type=jnp.float32
        )
        push = jnp.dot(
            neg_term.astype(jnp.bfloat16), memory_keys, preferred_element_type=jnp.float32
        )
        return (jnp.sum(pos_term, axis=1), jnp.sum(neg_term, axis=1), pull, push)

    pos_sum, neg_sum, pull, push = lax.map(
        score_block,
        (anchors.reshape(blocks, block_rows, width), labels_all.reshape(blocks, block_rows)),
    )
    pos_sum = pos_sum.reshape(row_count)
    neg_sum = neg_sum.reshape(row_count)
    pull = pull.reshape(row_count, width)
    push = push.reshape(row_count, width)
    pos_total, neg_total = lax.psum((pos_sum, neg_sum), ("grp", "dev"))
    combined = push / (1.0 + neg_total)[:, None] - pull / (1.0 + pos_total)[:, None]
    grad_unit = lax.psum_scatter(combined, ("grp", "dev"), scatter_dimension=0, tiled=True)
    own_pos = lax.dynamic_slice_in_dim(pos_total, my_index * local_rows, local_rows, 0)
    own_neg = lax.dynamic_slice_in_dim(neg_total, my_index * local_rows, local_rows, 0)
    anchor_loss = jnp.log(1.0 + own_pos) / pos_scale + jnp.log(1.0 + own_neg) / neg_scale
    along = jnp.sum(unit_rows * grad_unit, axis=1, keepdims=True)
    grad_batch = (grad_unit - unit_rows * along) / radius
    step_value = step_index[0]
    slot_index = step_value % (memory.shape[0] // local_rows)
    source = (my_index - step_value) % devices_all
    moved_rows = lax.dynamic_slice_in_dim(anchors, source * local_rows, local_rows, 0)
    moved_labels = lax.dynamic_slice_in_dim(labels_all, source * local_rows, local_rows, 0)
    new_memory = lax.dynamic_update_slice_in_dim(memory, moved_rows, slot_index * local_rows, 0)
    new_labels = lax.dynamic_update_slice_in_dim(
        memory_labels, moved_labels, slot_index * local_rows, 0
    )
    return (grad_batch, anchor_loss, new_memory, new_labels)


def solution(mesh):
    placed = (
        P(("grp", "dev"), None),
        P(("grp", "dev")),
        P(("grp", "dev"), None),
        P(("grp", "dev")),
        P(("grp", "dev")),
        P(),
    )
    return jax.shard_map(
        per_device,
        mesh=mesh,
        in_specs=placed,
        out_specs=(
            P(("grp", "dev"), None),
            P(("grp", "dev")),
            P(("grp", "dev"), None),
            P(("grp", "dev")),
        ),
        check_vma=False,
    )
```

profile of v0, /device:TPU:0, one launch (start us, length us, event | category | flops | bytes accessed | tf_op | source)
XLA Modules:
  0.0 900.4 jit_solution(15822129743591129531)
XLA Ops:
  10.1 68.7 %all-reduce = s32[4096]{0:T(1024)S(1)} all-reduce(s32[4096]{0:T(1024)S(1)} %dynamic-update-slice), channel_id=1, replica_groups=mesh['grp'=8,'dev'=16] {'grp','dev'}, use_global_device_ids=true, to_apply=%add | all-reduce | flops 4096 | bytes 32768
  81.1 81.6 %while.18 = (s32[]{:T(128)}, f32[8,512]{1,0:T(8,128)S(1)}, f32[8,512]{1,0:T(8,128)S(1)}, f32[8,512,512]{2,1,0:T(8,128)}, f32[8,512,512]{2,1,0:T(8,128)}, /*index...) while((s32[]{:T(128)}, f32[8,512]{1,0:T(8,128)S(1)}, ...), condition=%wide.region_5.6_spmd, body=%wide.region_2.5_spmd.sunk | while | flops 3246390272 | bytes 29943460 | solution.py:53
  81.2 5.1 fusion.60
  86.3 2.5 fusion.61
  88.8 2.5 fusion.62
  91.5 5.1 fusion.60
  98.9 2.5 fusion.62
  101.7 5.1 fusion.60
  109.1 2.5 fusion.62
  111.8 5.1 fusion.60
  119.3 2.5 fusion.62
  122.0 5.1 fusion.60
  127.1 2.4 fusion.61
  129.6 2.5 fusion.62
  132.2 5.1 fusion.60
  139.7 2.5 fusion.62
  142.4 5.1 fusion.60
  149.9 2.5 fusion.62
  152.6 5.1 fusion.60
  157.7 2.4 fusion.61
  160.1 2.5 fusion.62
  162.8 63.2 %all-reduce.1 = (f32[4096]{0:T(1024)S(1)}, f32[4096]{0:T(1024)S(1)}) all-reduce(f32[4096]{0:T(1024)S(1)} %bitcast.56, f32[4096]{0:T(1024)S(1)} %bitcast.55), channel_id=1, replica_groups=mesh['grp'=8,'dev'=16] {'grp','dev'}, use_global_device_ids=true, to_apply=%region_7.8 | all-reduce | flops 8192 | bytes 65536 | tf_op jit(solution)/shard_map/psum | solution.py:61
  225.9 10.1 %fusion.39 = f32[4096,512]{1,0:T(8,128)} fusion(f32[8,512,512]{2,1,0:T(8,128)} %get-tuple-element.134, f32[8,512,512]{2,1,0:T(8,128)} %get-tuple-element.132, f32[4096]{0:T(1024)S(1)} %get-tuple-element.161, f32[4096]{0:T(1024)S(1)} %get-tuple-element.162), kind=kLoop, calls=%fused_computation.35 | loop fusion | flops 6291456 | bytes 25198592 | tf_op jit(solution)/shard_map/sub | solution.py:62
  238.2 652.8 %reduce-scatter.2.cloned.1.call-done = f32[32,512]{1,0:T(8,128)} async-done(((f32[4096,512]{1,0:T(8,128)}), f32[32,512]{1,0:T(8,128)}) %reduce-scatter.2.cloned.1.call-update) | async-done | bytes 65552 | tf_op jit(solution)/shard_map/reduce_scatter | solution.py:63
  (94 shorter events, 22.2 us)
Async XLA Ops:
  7.2 1.7 copy-start.2
  7.2 2.6 copy-start.6
  7.2 71.6 %copy-start.3 = (s32[2048]{0:T(1024)S(1)}, s32[2048]{0:T(1024)}, u32[]{:S(2)}) copy-start(s32[2048]{0:T(1024)} %param.12) | copy-start | bytes 24580
  7.2 73.9 %all-gather.2.cloned.1.call-start = ((), (), s32[]{:S(2)}) async-start(), calls=%async_computation.1 | async-start | bytes 4227072 | tf_op jit(solution)/shard_map/all_gather | solution.py:26
  8.8 72.3 %copy-start.5 = (s32[2048]{0:T(1024)S(1)}, s32[2048]{0:T(1024)}, u32[]{:S(2)}) copy-start(s32[2048]{0:T(1024)} %param.11) | copy-start | bytes 24580
  9.7 881.3 %reduce-scatter.2.cloned.1.call-start = ((), (), s32[]{:S(2)}) async-start(), calls=%async_computation.2 | async-start | bytes 8454144 | tf_op jit(solution)/shard_map/reduce_scatter | solution.py:63
  81.2 5.1 copy-start.1
  91.4 5.1 copy-start.1
  101.7 5.1 copy-start.1
  111.8 5.1 copy-start.1
  122.0 5.1 copy-start.1
  132.2 5.1 copy-start.1
  142.4 5.1 copy-start.1
  152.6 5.1 copy-start.1
  237.4 656.2 %copy-start.4 = (s32[2048]{0:T(1024)}, s32[2048]{0:T(1024)S(1)}, u32[]{:S(2)}) copy-start(s32[2048]{0:T(1024)S(1)} %dynamic-slice_dynamic-update-slice_fusion.1) | copy-start | bytes 24580
  238.2 655.4 %copy-start = (bf16[2048,512]{1,0:T(8,128)(2,1)}, bf16[2048,512]{1,0:T(8,128)(2,1)S(1)}, u32[]{:S(2)}) copy-start(bf16[2048,512]{1,0:T(8,128)(2,1)S(1)} %dynamic-slice_dynamic-update-slice_fusion) | copy-start | bytes 6291460
Sparse Core Ops, SparseCore 0:
  11.7 69.2 all-gather.1
  236.1 654.8 reduce-scatter.1
where the time goes:
time: 901 us; the launch traced here: 900 us
  waiting for transfers between devices  653 us (72%)
  blocking collectives  132 us (15%)
  matrix products  80 us (9%)
  other arithmetic  16.7 us (2%)
  between operations  14.9 us (2%)
    reduce_scatter x1, waiting for transfers between devices, per_device(): lax.psum_scatter(combined, ('grp', 'dev'), scatter_dimension=0, tiled=True)  653 us
    unnamed x1, blocking collectives  68.7 us
    psum x1, blocking collectives, per_device(): pos_total, neg_total = lax.psum((pos_sum, neg_sum), ('grp', 'dev'))  63.2 us
    dot_general x8, matrix products, score_block(): lax.dot_general(block_anchors, memory_keys, (((1,), (1,)), ((), ())), pre...  40.9 us
    dot_general x8, matrix products, score_block(): jnp.dot(neg_term.astype(jnp.bfloat16), memory_keys, preferred_element_typ...  20.1 us
    dot_general x8, matrix products, score_block(): jnp.dot(pos_term.astype(jnp.bfloat16), memory_keys, preferred_element_typ...  19.1 us
  transfers between devices with their start and end apart: 2, of which 1 were waited for; matrix products, arithmetic and copies ran while one was open for 0% of the time, Pallas kernels for 0%

commit v1 on v0

--- a/solution.py
+++ b/solution.py
@@ -58,7 +58,7 @@
     neg_sum = neg_sum.reshape(row_count)
     pull = pull.reshape(row_count, width)
     push = push.reshape(row_count, width)
-    pos_total, neg_total = lax.psum((pos_sum, neg_sum), ("grp", "dev"))
+    pos_total, neg_total = lax.psum(lax.psum((pos_sum, neg_sum), "grp"), "dev")
     combined = push / (1.0 + neg_total)[:, None] - pull / (1.0 + pos_total)[:, None]
     grad_unit = lax.psum_scatter(combined, ("grp", "dev"), scatter_dimension=0, tiled=True)
     own_pos = lax.dynamic_slice_in_dim(pos_total, my_index * local_rows, local_rows, 0)

time: 901 us -> 927 us (1.029)
  blocking collectives: 132 us -> 161 us
    psum x1 -> x2, blocking collectives: 63.2 us -> 92.4 us  [per_device(): pos_total, neg_total = lax.psum(lax.psum((pos_sum, neg_sum), 'grp'), 'dev')]
where the time goes in v1:
time: 927 us; the launch traced here: 926 us
  waiting for transfers between devices  649 us (70%)
  blocking collectives  161 us (17%)
  matrix products  80.1 us (9%)
  other arithmetic  16.7 us (2%)
  between operations  14.9 us (2%)
    reduce_scatter x1, waiting for transfers between devices, per_device(): lax.psum_scatter(combined, ('grp', 'dev'), scatter_dimension=0, tiled=True)  649 us
    psum x2, blocking collectives, per_device(): pos_total, neg_total = lax.psum(lax.psum((pos_sum, neg_sum), 'grp'), 'dev')  92.4 us
    unnamed x1, blocking collectives  68.7 us
    dot_general x8, matrix products, score_block(): lax.dot_general(block_anchors, memory_keys, (((1,), (1,)), ((), ())), pre...  40.9 us
    dot_general x8, matrix products, score_block(): jnp.dot(neg_term.astype(jnp.bfloat16), memory_keys, preferred_element_typ...  20.1 us
    dot_general x8, matrix products, score_block(): jnp.dot(pos_term.astype(jnp.bfloat16), memory_keys, preferred_element_typ...  19.1 us
  transfers between devices with their start and end apart: 2, of which 1 were waited for; matrix products, arithmetic and copies ran while one was open for 0% of the time, Pallas kernels for 0%

profile of v1, /device:TPU:0, one launch (start us, length us, event | category | flops | bytes accessed | tf_op | source)
XLA Modules:
  0.0 926.3 jit_solution(3112915667023823857)
XLA Ops:
  10.1 68.7 %all-reduce = s32[4096]{0:T(1024)S(1)} all-reduce(s32[4096]{0:T(1024)S(1)} %dynamic-update-slice), channel_id=1, replica_groups=mesh['grp'=8,'dev'=16] {'grp','dev'}, use_global_device_ids=true, to_apply=%add | all-reduce | flops 4096 | bytes 32768
  81.1 81.6 %while.18 = (s32[]{:T(128)}, f32[8,512]{1,0:T(8,128)S(1)}, f32[8,512]{1,0:T(8,128)S(1)}, f32[8,512,512]{2,1,0:T(8,128)}, f32[8,512,512]{2,1,0:T(8,128)}, /*index...) while((s32[]{:T(128)}, f32[8,512]{1,0:T(8,128)S(1)}, ...), condition=%wide.region_5.6_spmd, body=%wide.region_2.5_spmd.sunk | while | flops 3246390272 | bytes 29943460 | solution.py:53
  81.2 5.1 fusion.60
  86.3 2.5 fusion.61
  88.8 2.5 fusion.62
  91.5 5.1 fusion.60
  98.9 2.5 fusion.62
  101.7 5.1 fusion.60
  109.2 2.5 fusion.62
  111.9 5.1 fusion.60
  119.3 2.5 fusion.62
  122.0 5.1 fusion.60
  127.1 2.4 fusion.61
  129.6 2.5 fusion.62
  132.2 5.1 fusion.60
  139.7 2.5 fusion.62
  142.4 5.1 fusion.60
  149.9 2.5 fusion.62
  152.6 5.1 fusion.60
  160.1 2.5 fusion.62
  162.8 39.5 %all-reduce.2 = (f32[4096]{0:T(1024)S(1)}, f32[4096]{0:T(1024)S(1)}) all-reduce(f32[4096]{0:T(1024)S(1)} %bitcast.56, f32[4096]{0:T(1024)S(1)} %bitcast.55), channel_id=1, replica_groups=mesh['grp'=8,'dev'=16] {'grp'}, use_global_device_ids=true, to_apply=%region_8.9 | all-reduce | flops 8192 | bytes 65536 | tf_op jit(solution)/shard_map/psum | solution.py:61
  202.3 52.9 %all-reduce.1 = (f32[4096]{0:T(1024)S(1)}, f32[4096]{0:T(1024)S(1)}) all-reduce(f32[4096]{0:T(1024)S(1)} %get-tuple-element.160, f32[4096]{0:T(1024)S(1)} %get-tuple-element.161), channel_id=1, replica_groups=mesh['grp'=8,'dev'=16] {'dev'}, use_global_device_ids=true, to_apply=%region_9.10 | all-reduce | flops 8192 | bytes 65536 | tf_op jit(solution)/shard_map/psum | solution.py:61
  255.2 10.0 %fusion.39 = f32[4096,512]{1,0:T(8,128)} fusion(f32[8,512,512]{2,1,0:T(8,128)} %get-tuple-element.134, f32[8,512,512]{2,1,0:T(8,128)} %get-tuple-element.132, f32[4096]{0:T(1024)S(1)} %get-tuple-element.163, f32[4096]{0:T(1024)S(1)} %get-tuple-element.164), kind=kLoop, calls=%fused_computation.35 | loop fusion | flops 6291456 | bytes 25198592 | tf_op jit(solution)/shard_map/sub | solution.py:62
  267.5 649.4 %reduce-scatter.2.cloned.1.call-done = f32[32,512]{1,0:T(8,128)} async-done(((f32[4096,512]{1,0:T(8,128)}), f32[32,512]{1,0:T(8,128)}) %reduce-scatter.2.cloned.1.call-update) | async-done | bytes 65552 | tf_op jit(solution)/shard_map/reduce_scatter | solution.py:63
  (95 shorter events, 24.6 us)
Async XLA Ops:
  7.2 1.7 copy-start.2
  7.2 2.6 copy-start.6
  7.2 71.6 %copy-start.3 = (s32[2048]{0:T(1024)S(1)}, s32[2048]{0:T(1024)}, u32[]{:S(2)}) copy-start(s32[2048]{0:T(1024)} %param.12) | copy-start | bytes 24580
  7.2 73.9 %all-gather.2.cloned.1.call-start = ((), (), s32[]{:S(2)}) async-start(), calls=%async_computation.1 | async-start | bytes 4227072 | tf_op jit(solution)/shard_map/all_gather | solution.py:26
  8.8 72.3 %copy-start.5 = (s32[2048]{0:T(1024)S(1)}, s32[2048]{0:T(1024)}, u32[]{:S(2)}) copy-start(s32[2048]{0:T(1024)} %param.11) | copy-start | bytes 24580
  9.7 907.2 %reduce-scatter.2.cloned.1.call-start = ((), (), s32[]{:S(2)}) async-start(), calls=%async_computation.2 | async-start | bytes 8454144 | tf_op jit(solution)/shard_map/reduce_scatter | solution.py:63
  81.2 5.1 copy-start.1
  91.5 5.1 copy-start.1
  101.7 5.1 copy-start.1
  111.8 5.1 copy-start.1
  122.0 5.1 copy-start.1
  132.2 5.1 copy-start.1
  142.4 5.1 copy-start.1
  152.6 5.1 copy-start.1
  266.7 652.7 %copy-start.4 = (s32[2048]{0:T(1024)}, s32[2048]{0:T(1024)S(1)}, u32[]{:S(2)}) copy-start(s32[2048]{0:T(1024)S(1)} %dynamic-slice_dynamic-update-slice_fusion.1) | copy-start | bytes 24580
  267.5 652.0 %copy-start = (bf16[2048,512]{1,0:T(8,128)(2,1)}, bf16[2048,512]{1,0:T(8,128)(2,1)S(1)}, u32[]{:S(2)}) copy-start(bf16[2048,512]{1,0:T(8,128)(2,1)S(1)} %dynamic-slice_dynamic-update-slice_fusion) | copy-start | bytes 6291460
Sparse Core Ops, SparseCore 0:
  11.7 69.2 all-gather.1
  265.4 651.4 reduce-scatter.1
